TPU v7x, 128 devices: a whole 4x4x4 slice. The times are simulated.
128 devices in a mesh: rep: 8 (over z, core), tensor: 16 (over y, x).
Axes of the slice: x: 4, y: 4, z: 4, core: 2. Of those that a mesh axis runs over, the one named last changes fastest.
Arguments:
- x_pre: bfloat16 [8192, 2560], P(('rep', 'tensor')), may hold values from -6 to 6
- x_dec: bfloat16 [16, 2560], replicated, may hold values from -6 to 6
- prefix_kv: bfloat16 [8, 4096, 32, 160], P('rep', None, 'tensor'), may hold values from -400 to 400
- cache_kv: bfloat16 [16, 4096, 32, 160], P(None, 'rep', 'tensor'), may hold values from -400 to 400
- dec_len: int32 [16], replicated, may hold values from 1 to 4096, as said below
- offsets: int32 [8], P('rep'), may hold values from 0 to 4096, as said below
- segments: int32 [8, 1024], P('rep'), may hold values from 0 to 3, never falling along the last dimension, each value on 1 to 512 neighbouring positions
- w_qkv: bfloat16 [2560, 7680], P(None, 'tensor'), may hold values from -0.125 to 0.125
- w_out: bfloat16 [2560, 2560], P('tensor'), may hold values from -0.125 to 0.125
- w_up: bfloat16 [2560, 10240], P(None, 'tensor'), may hold values from -0.125 to 0.125
- up_bias: float32 [10240], P('tensor'), may hold values from -3 to 3
- w_down: bfloat16 [10240, 2560], P('tensor'), may hold values from -0.0625 to 0.0625
- biases: float32 [2, 2560], replicated, may hold values from -3 to 3
- gains: float32 [2, 2560], replicated, may hold values from 0.1 to 1.9
- shifts: float32 [2, 2560], replicated, may hold values from -2.5 to 2.5
- w_next: bfloat16 [2560, 7680], P(None, 'tensor'), may hold values from -0.125 to 0.125
Outputs:
- layer_out: bfloat16 [8192, 2560], P(('rep', 'tensor'))
- next_qkv: bfloat16 [8192, 7680], P('rep', 'tensor')
- dec_out: bfloat16 [16, 2560], replicated
- dec_next_qkv: bfloat16 [16, 7680], P(None, 'tensor')
Inputs may be any that keep to these rules, and one draw needn't show every extreme that they name: Request r's cache holds live entries at positions below dec_len[r]; in every draw one request's cache is full (4096) and one request has a single live position. `offsets`: in every draw one span has a full earlier cache (4096 positions) and one span has none.
All inputs are finite; a program needn't handle non-finite values.
Results may differ from a plain program's by a relative error of at most 0.025.
Values may be sent and summed in bfloat16 or wider, within the bound.
A program may use at most 192 MiB of HBM per device.

v0:
```python
import jax
import jax.numpy as jnp
from jax import lax
from jax.sharding import PartitionSpec as P

NEG = -1e30


def combined_all(value, axis, join):
    pieces = jax.tree.map(lambda part: lax.all_gather(part, axis), value)
    head = jax.tree.map(lambda part: part[0], pieces)
    tail = jax.tree.map(lambda part: part[1:], pieces)
    total, _ = lax.scan(lambda total, slab: (join(total, slab), None), head, tail)
    return total


def layer_norm(values, gain_row, shift_row):
    average = jnp.mean(values, axis=-1, keepdims=True)
    centred = values - average
    spread = jnp.mean(centred * centred, axis=-1, keepdims=True)
    return centred * lax.rsqrt(spread + 1e-05) * gain_row + shift_row


def visible(seg_query, query_pos, seg_all, offset, prefix_len):
    prefix_pos = jnp.arange(prefix_len)
    from_prefix = (prefix_pos[None, :] < offset) & (seg_query[:, None] == 0)
    span_pos = jnp.arange(seg_all.shape[0])
    from_span = (seg_all[None, :] == seg_query[:, None]) & (span_pos[None, :] <= query_pos[:, None])
    return jnp.concatenate([from_prefix, from_span], axis=1)


def combine(earlier, later):
    high_early, total_early, output_early = earlier
    high_later, total_later, output_later = later
    highest = jnp.maximum(high_early, high_later)
    factor_early = jnp.exp(high_early - highest)
    factor_later = jnp.exp(high_later - highest)
    return (
        highest,
        total_early * factor_early + total_later * factor_later,
        output_early * factor_early[..., None] + output_later * factor_later[..., None],
    )


def block_state(queries, keys, values, valid, scale):
    scores = jnp.einsum("rhd,rphd->rhp", queries, keys, preferred_element_type=jnp.float32) * scale
    scores = jnp.where(valid[:, None, :], scores, NEG)
    highest = jnp.max(scores, axis=-1)
    weights = jnp.where(valid[:, None, :], jnp.exp(scores - highest[..., None]), 0.0)
    totals = jnp.sum(weights, axis=-1)
    output = jnp.einsum("rhp,rphd->rhd", weights, values.astype(jnp.float32))
    return (highest, totals, output)


def per_device(
    x_pre,
    x_dec,
    prefix_kv,
    cache_kv,
    dec_len,
    offsets,
    segments,
    w_qkv,
    w_out,
    w_up,
    up_bias,
    w_down,
    biases,
    gains,
    shifts,
    w_next,
):
    heads_dev = prefix_kv.shape[2]
    head_dim = prefix_kv.shape[3] // 2
    prefix_len = prefix_kv.shape[1]
    span_len = segments.shape[1]
    scale = head_dim ** (-0.5)

    def up_rows(piece):
        return jax.nn.gelu(
            jnp.dot(piece, w_up, preferred_element_type=jnp.float32) + up_bias, approximate=False
        ).astype(jnp.bfloat16)

    def next_rows(piece):
        return jnp.dot(piece, w_next, preferred_element_type=jnp.float32).astype(jnp.bfloat16)

    qkv_all = jnp.dot(
        lax.all_gather(x_pre, "tensor", axis=0, tiled=True),
        w_qkv,
        preferred_element_type=jnp.float32,
    ).astype(jnp.bfloat16)
    dec_qkv = jnp.dot(x_dec, w_qkv, preferred_element_type=jnp.float32).astype(jnp.bfloat16)
    dec_four = dec_qkv.reshape(dec_qkv.shape[0], heads_dev, 3, head_dim)
    dec_query = dec_four[:, :, 0]
    positions = cache_kv.shape[1]
    cache_base = lax.axis_index("rep") * positions
    valid = (cache_base + jnp.arange(positions))[None, :] < dec_len[:, None]
    state = block_state(dec_query, cache_kv[..., :head_dim], cache_kv[..., head_dim:], valid, scale)
    is_first = lax.axis_index("rep") == 0
    own_score = (
        jnp.sum(dec_query.astype(jnp.float32) * dec_four[:, :, 1].astype(jnp.float32), axis=-1)
        * scale
    )
    own_state = (
        jnp.where(is_first, own_score, NEG),
        jnp.where(is_first, jnp.ones_like(own_score), jnp.zeros_like(own_score)),
        jnp.where(is_first, dec_four[:, :, 2].astype(jnp.float32), 0.0),
    )
    state = combine(state, own_state)
    merged = combined_all(state, "rep", combine)
    dec_attn = (
        (merged[2] / merged[1][..., None])
        .astype(jnp.bfloat16)
        .reshape(dec_qkv.shape[0], heads_dev * head_dim)
    )
    qkv_four = qkv_all.reshape(span_len, heads_dev, 3, head_dim)
    queries = qkv_four[:, :, 0]
    prefix = prefix_kv[0]
    keys = jnp.concatenate([prefix[:, :, :head_dim], qkv_four[:, :, 1]], axis=0)
    values = jnp.concatenate([prefix[:, :, head_dim:], qkv_four[:, :, 2]], axis=0)
    seg_all = segments[0]
    offset = offsets[0]
    query_block = min(512, span_len)

    def attend_block(index):
        begin = index * query_block
        query_rows = lax.dynamic_slice_in_dim(queries, begin, query_block, 0)
        seg_query = lax.dynamic_slice_in_dim(seg_all, begin, query_block, 0)
        mask = visible(seg_query, begin + jnp.arange(query_block), seg_all, offset, prefix_len)
        scores = (
            jnp.einsum("qhd,khd->hqk", query_rows, keys, preferred_element_type=jnp.float32) * scale
        )
        scores = jnp.where(mask[None], scores, NEG)
        highest = jnp.max(scores, axis=-1, keepdims=True)
        weights = jnp.where(mask[None], jnp.exp(scores - highest), 0.0)
        weights = (weights / jnp.sum(weights, axis=-1, keepdims=True)).astype(jnp.bfloat16)
        return jnp.einsum(
            "hqk,khd->qhd", weights, values, preferred_element_type=jnp.float32
        ).astype(jnp.bfloat16)

    blocks = lax.map(attend_block, jnp.arange(span_len // query_block))
    attn = blocks.reshape(span_len, heads_dev * head_dim)
    attn_part = lax.psum_scatter(
        jnp.dot(attn, w_out, preferred_element_type=jnp.float32).astype(jnp.bfloat16),
        "tensor",
        scatter_dimension=0,
        tiled=True,
    ).astype(jnp.float32)
    dec_sum = lax.psum(
        jnp.dot(dec_attn, w_out, preferred_element_type=jnp.float32).astype(jnp.bfloat16), "tensor"
    ).astype(jnp.float32)
    h_first = layer_norm(
        x_pre.astype(jnp.float32) + attn_part + biases[0], gains[0], shifts[0]
    ).astype(jnp.bfloat16)
    hidden = up_rows(lax.all_gather(h_first, "tensor", axis=0, tiled=True))
    dec_first = layer_norm(
        x_dec.astype(jnp.float32) + dec_sum + biases[0], gains[0], shifts[0]
    ).astype(jnp.bfloat16)
    mlp_part = lax.psum_scatter(
        jnp.dot(hidden, w_down, preferred_element_type=jnp.float32).astype(jnp.bfloat16),
        "tensor",
        scatter_dimension=0,
        tiled=True,
    ).astype(jnp.float32)
    layer_out = layer_norm(
        h_first.astype(jnp.float32) + mlp_part + biases[1], gains[1], shifts[1]
    ).astype(jnp.bfloat16)
    dec_hidden = up_rows(dec_first)
    dec_mlp = lax.psum(
        jnp.dot(dec_hidden, w_down, preferred_element_type=jnp.float32).astype(jnp.bfloat16),
        "tensor",
    ).astype(jnp.float32)
    dec_out = layer_norm(
        dec_first.astype(jnp.float32) + dec_mlp + biases[1], gains[1], shifts[1]
    ).astype(jnp.bfloat16)
    next_qkv = next_rows(lax.all_gather(layer_out, "tensor", axis=0, tiled=True))
    dec_next_qkv = next_rows(dec_out)
    return (layer_out, next_qkv, dec_out, dec_next_qkv)


def solution(mesh):
    placed = (
        P(("rep", "tensor"), None),
        P(),
        P("rep", None, "tensor", None),
        P(None, "rep", "tensor", None),
        P(),
        P("rep"),
        P("rep", None),
        P(None, "tensor"),
        P("tensor", None),
        P(None, "tensor"),
        P("tensor"),
        P("tensor", None),
        P(),
        P(),
        P(),
        P(None, "tensor"),
    )
    return jax.shard_map(
        per_device,
        mesh=mesh,
        in_specs=placed,
        out_specs=(P(("rep", "tensor"), None), P("rep", "tensor"), P(), P(None, "tensor")),
        check_vma=False,
    )
```

profile of v0, /device:TPU:1, one launch (start us, length us, event | category | flops | bytes accessed | tf_op | source)
XLA Modules:
  0.0 648.3 jit_solution(16715024463593659003)
XLA Ops:
  8.0 3.7 fusion.182
  11.7 58.0 %all-gather.5.cloned.1.call-done = bf16[1024,2560]{1,0:T(8,128)(2,1)} async-done(((bf16[64,2560]{1,0:T(8,128)(2,1)}), bf16[1024,2560]{1,0:T(8,128)(2,1)}) %all-gather.5.cloned.1.call-update) | async-done | bytes 5242896 | tf_op jit(solution)/shard_map/all_gather | solution.py:88
  69.7 6.1 convolution_convert_fusion.5
  79.2 101.0 %while.24 = (s32[]{:T(128)}, bf16[2,512,2,80]{1,3,2,0:T(8,128)(2,1)}, s32[]{:T(128)}, s32[2]{0:T(128)S(1)}, s32[1024]{0:T(1024)S(1)}, /*index=5*/s32[1,1024]{1,0...) while((s32[]{:T(128)}, ...), condition=%wide.region_3.4_spmd, body=%wide.region_0.3_spmd.sunk | while | flops 1731291136 | bytes 107183400 | solution.py:141
  80.4 11.4 %fusion.215 = f32[2,512,5120]{2,1,0:T(8,128)} fusion(bf16[5120,2,80]{0,2,1:T(8,128)(2,1)} %get-tuple-element.300, bf16[1024,2,80]{0,2,1:T(8,128)(2,1)} %get-tuple-element.299, s32[]{:T(128)S(6)} %select_n.124), kind=kOutput, calls=%fused_computation.16.clone.1 | convolution fusion | flops 838860800 | bytes 22773764 | tf_op jit(solution)/shard_map/while/body/eval_jaxpr/qhd,khd->hqk/dot_general | solution.py:131
  94.7 25.4 %fusion.217 = (f32[2,512]{1,0:T(2,128)S(1)}, f32[2,512,5120]{2,1,0:T(8,128)}) fusion(f32[2,512,5120]{2,1,0:T(8,128)} %fusion.215, pred[512,5120]{1,0:T(8,128)(4,1)S(1)} %pad_add_fusion.2), kind=kOutput, calls=%fused_computation.273.clone.1 | output fusion | flops 36705280 | bytes 44568576 | tf_op jit(solution)/shard_map/while/body/eval_jaxpr/sub | solution.py:135
  120.1 8.8 %fusion.218 = bf16[2,512,2,80]{1,3,2,0:T(8,128)(2,1)S(1)} fusion(bf16[2,512,2,80]{1,3,2,0:T(8,128)(2,1)S(1)} %copy-done.6, s32[]{:T(128)S(6)} %copy.93, bf16[5120,2,80]{0,2,1:T(8,128)(2,1)S(1)} %copy-done.3, f32[2,512,5120]{2,1,0:T(8,128)} %get-tuple-element.254, f32[2,512]{1,0:T(2,128)S(1)} %get-tuple-element.255), kind=kOutput, calls=%fused_computation.15.clone.1 | convolution fusion | flops 849428480 | bytes 22777860 | tf_op jit(solution)/shard_map/while/body/eval_jaxpr/hqk,khd->qhd/dot_general | solution.py:137
  130.9 11.4 %fusion.215 = f32[2,512,5120]{2,1,0:T(8,128)} fusion(bf16[5120,2,80]{0,2,1:T(8,128)(2,1)} %get-tuple-element.300, bf16[1024,2,80]{0,2,1:T(8,128)(2,1)} %get-tuple-element.299, s32[]{:T(128)S(6)} %select_n.124), kind=kOutput, calls=%fused_computation.16.clone.1 | convolution fusion | flops 838860800 | bytes 22773764 | tf_op jit(solution)/shard_map/while/body/eval_jaxpr/qhd,khd->hqk/dot_general | solution.py:131
  145.2 25.4 %fusion.217 = (f32[2,512]{1,0:T(2,128)S(1)}, f32[2,512,5120]{2,1,0:T(8,128)}) fusion(f32[2,512,5120]{2,1,0:T(8,128)} %fusion.215, pred[512,5120]{1,0:T(8,128)(4,1)S(1)} %pad_add_fusion.2), kind=kOutput, calls=%fused_computation.273.clone.1 | output fusion | flops 36705280 | bytes 44568576 | tf_op jit(solution)/shard_map/while/body/eval_jaxpr/sub | solution.py:135
  170.6 8.8 %fusion.218 = bf16[2,512,2,80]{1,3,2,0:T(8,128)(2,1)S(1)} fusion(bf16[2,512,2,80]{1,3,2,0:T(8,128)(2,1)S(1)} %copy-done.6, s32[]{:T(128)S(6)} %copy.93, bf16[5120,2,80]{0,2,1:T(8,128)(2,1)S(1)} %copy-done.3, f32[2,512,5120]{2,1,0:T(8,128)} %get-tuple-element.254, f32[2,512]{1,0:T(2,128)S(1)} %get-tuple-element.255), kind=kOutput, calls=%fused_computation.15.clone.1 | convolution fusion | flops 849428480 | bytes 22777860 | tf_op jit(solution)/shard_map/while/body/eval_jaxpr/hqk,khd->qhd/dot_general | solution.py:137
  181.5 5.0 convolution_convert_fusion.1
  187.4 76.8 %reduce-scatter.3.cloned.1.call-done = bf16[64,2560]{1,0:T(8,128)(2,1)} async-done(((bf16[1024,2560]{1,0:T(8,128)(2,1)}), bf16[64,2560]{1,0:T(8,128)(2,1)}) %reduce-scatter.3.cloned.1.call-update) | async-done | bytes 327696 | tf_op jit(solution)/shard_map/reduce_scatter | solution.py:143
  279.1 14.9 %all-gather = f32[128,2,80]{2,1,0:T(2,128)S(1)} all-gather(f32[16,2,80]{2,1,0:T(2,128)S(1)} %multiply_add_fusion), channel_id=2, replica_groups=mesh['rep'=8,'tensor'=16] {'rep'}, dimensions={0}, use_global_device_ids=true | all-gather | bytes 92160 | tf_op jit(solution)/shard_map/all_gather | solution.py:10
  296.2 10.2 %all_gather.26 = f32[8,16,2]{1,2,0:T(2,128)S(1)} all-gather(f32[1,16,2]{1,2,0:T(2,128)S(1)} %get-tuple-element.148), channel_id=1, replica_groups=mesh['rep'=8,'tensor'=16] {'rep'}, dimensions={0}, use_global_device_ids=true | all-gather | bytes 1152 | tf_op jit(solution)/shard_map/all_gather | solution.py:10
  306.4 8.1 %all_gather.27 = f32[8,16,2]{1,2,0:T(2,128)S(1)} all-gather(f32[1,16,2]{1,2,0:T(2,128)S(1)} %get-tuple-element.147), channel_id=1, replica_groups=mesh['rep'=8,'tensor'=16] {'rep'}, dimensions={0}, use_global_device_ids=true | all-gather | bytes 1152 | tf_op jit(solution)/shard_map/all_gather | solution.py:10
  314.5 7.4 %while.25 = (s32[]{:T(128)}, f32[16,2]{0,1:T(2,128)S(1)}, f32[16,2]{0,1:T(2,128)S(1)}, f32[16,2,80]{2,1,0:T(2,128)S(1)}, f32[7,16,2]{1,2,0:T(2,128)S(1)}, /*inde...) while((s32[]{:T(128)}, f32[16,2]{0,1:T(2,128)S(1)}, f32[16,2]{0,1:T(2,128)S(1)}, ...), condition=%wide.region_14.15_spmd, body=%wide.region_13.14_spmd.sunk | while | flops 7874 | bytes 32613 | solution.py:13
  325.7 17.9 %convolution_convert_fusion = bf16[1024,2560]{1,0:T(8,128)(2,1)} fusion(bf16[640,2560]{1,0:T(8,128)(2,1)S(1)} %copy-done, bf16[1024,2560]{1,0:T(8,128)(2,1)} %all-gather.7.cloned.1.call-done, bf16[2560,640]{1,0:T(8,128)(2,1)} %param.29, f32[640]{0:T(1024)} %param.30), kind=kOutput, calls=%fused_computation.33 | convolution fusion | flops 6756761600 | bytes 17041920 | tf_op jit(solution)/shard_map/dot_general | solution.py:160
  343.8 64.3 %all-reduce.3.cloned.1.call-done = bf16[16,2560]{1,0:T(8,128)(2,1)} async-done(((bf16[16,2560]{1,0:T(8,128)(2,1)}), bf16[16,2560]{1,0:T(8,128)(2,1)}) %all-reduce.3.cloned.1.call-update) | async-done | bytes 81936 | tf_op jit(solution)/shard_map/psum | solution.py:149
  411.2 3.6 convolution_convert_fusion.2
  414.9 75.9 %reduce-scatter.5.cloned.1.call-done = bf16[64,2560]{1,0:T(8,128)(2,1)} async-done(((bf16[1024,2560]{1,0:T(8,128)(2,1)}), bf16[64,2560]{1,0:T(8,128)(2,1)}) %reduce-scatter.5.cloned.1.call-update) | async-done | bytes 327696 | tf_op jit(solution)/shard_map/reduce_scatter | solution.py:159
  495.4 78.8 %all-reduce.5.cloned.1.call-done = bf16[16,2560]{1,0:T(8,128)(2,1)} async-done(((bf16[16,2560]{1,0:T(8,128)(2,1)}), bf16[16,2560]{1,0:T(8,128)(2,1)}) %all-reduce.5.cloned.1.call-update) | async-done | bytes 81936 | tf_op jit(solution)/shard_map/psum | solution.py:169
  577.4 3.1 convolution_convert_fusion.6
  580.5 54.0 %all-gather.9.cloned.1.call-done = bf16[1024,2560]{1,0:T(8,128)(2,1)} async-done(((bf16[64,2560]{1,0:T(8,128)(2,1)}), bf16[1024,2560]{1,0:T(8,128)(2,1)}) %all-gather.9.cloned.1.call-update) | async-done | bytes 5242896 | tf_op jit(solution)/shard_map/all_gather | solution.py:176
  634.5 6.9 %convolution_convert_fusion.4 = bf16[1024,480]{0,1:T(8,128)(2,1)} fusion(bf16[1024,2560]{1,0:T(8,128)(2,1)} %all-gather.9.cloned.1.call-done, bf16[2560,480]{0,1:T(8,128)(2,1)} %param.35), kind=kOutput, calls=%fused_computation.62 | convolution fusion | flops 2517073920 | bytes 8683520 | tf_op jit(solution)/shard_map/dot_general | solution.py:85
  (156 shorter events, 53.7 us)
Async XLA Ops:
  7.2 318.6 %copy-start = (bf16[640,2560]{1,0:T(8,128)(2,1)S(1)}, bf16[640,2560]{1,0:T(8,128)(2,1)}, u32[]{:S(2)}) copy-start(bf16[640,2560]{1,0:T(8,128)(2,1)} %param.31) | copy-start | bytes 9830404
  7.2 62.5 %all-gather.5.cloned.1.call-start = ((), (), s32[]{:S(2)}) async-start(), calls=%async_computation.2 | async-start | bytes 5570560 | tf_op jit(solution)/shard_map/all_gather | solution.py:88
  7.9 256.3 %reduce-scatter.3.cloned.1.call-start = ((), (), s32[]{:S(2)}) async-start(), calls=%async_computation.3 | async-start | bytes 5570560 | tf_op jit(solution)/shard_map/reduce_scatter | solution.py:143
  69.7 6.9 %copy-start.2 = (bf16[4096,2,80]{0,2,1:T(8,128)(2,1)S(1)}, bf16[4096,2,80]{0,2,1:T(8,128)(2,1)}, u32[]{:S(2)}) copy-start(bf16[4096,2,80]{0,2,1:T(8,128)(2,1)} %get-tuple-element.139) | copy-start | bytes 3932164
  75.7 1.4 copy-start.1
  77.2 2.0 copy-start.8
  94.7 25.4 %copy-start.3 = (bf16[5120,2,80]{0,2,1:T(8,128)(2,1)S(1)}, bf16[5120,2,80]{0,2,1:T(8,128)(2,1)}, u32[]{:S(2)}) copy-start(bf16[5120,2,80]{0,2,1:T(8,128)(2,1)} %get-tuple-element.301) | copy-start | bytes 4915204 | tf_op jit(solution)/shard_map/while
  94.7 25.4 %copy-start.6 = (bf16[2,512,2,80]{1,3,2,0:T(8,128)(2,1)S(1)}, bf16[2,512,2,80]{1,3,2,0:T(8,128)(2,1)}, u32[]{:S(2)}) copy-start(bf16[2,512,2,80]{1,3,2,0:T(8,128)(2,1)} %get-tuple-element.281) | copy-start | bytes 983044 | tf_op jit(solution)/shard_map/while
  145.1 25.4 %copy-start.3 = (bf16[5120,2,80]{0,2,1:T(8,128)(2,1)S(1)}, bf16[5120,2,80]{0,2,1:T(8,128)(2,1)}, u32[]{:S(2)}) copy-start(bf16[5120,2,80]{0,2,1:T(8,128)(2,1)} %get-tuple-element.301) | copy-start | bytes 4915204 | tf_op jit(solution)/shard_map/while
  145.2 25.4 %copy-start.6 = (bf16[2,512,2,80]{1,3,2,0:T(8,128)(2,1)S(1)}, bf16[2,512,2,80]{1,3,2,0:T(8,128)(2,1)}, u32[]{:S(2)}) copy-start(bf16[2,512,2,80]{1,3,2,0:T(8,128)(2,1)} %get-tuple-element.281) | copy-start | bytes 983044 | tf_op jit(solution)/shard_map/while
  186.5 0.8 copy-start.14
  186.6 82.6 %copy-start.4 = (bf16[16,2560]{1,0:T(8,128)(2,1)S(1)}, bf16[16,2560]{1,0:T(8,128)(2,1)}, u32[]{:S(2)}) copy-start(bf16[16,2560]{1,0:T(8,128)(2,1)} %param.21) | copy-start | bytes 245764
  186.6 139.2 %all-gather.7.cloned.1.call-start = ((), (), s32[]{:S(2)}) async-start(), calls=%async_computation.4 | async-start | bytes 5570560 | tf_op jit(solution)/shard_map/all_gather | solution.py:155
  264.2 8.4 %copy-start.17 = (s32[16]{0:T(128)S(1)}, s32[16]{0:T(128)}, u32[]{:S(2)}) copy-start(s32[16]{0:T(128)} %param.24) | copy-start | bytes 196
  268.9 139.2 %all-reduce.3.cloned.1.call-start = ((), (), s32[]{:S(2)}) async-start(), calls=%async_computation.7 | async-start | bytes 163840 | tf_op jit(solution)/shard_map/psum | solution.py:149
  272.6 2.4 copy-start.15
  274.9 4.0 copy-start.11
  276.3 2.6 copy-start.9
  276.3 2.7 copy-start.10
  324.2 166.5 %reduce-scatter.5.cloned.1.call-start = ((), (), s32[]{:S(2)}) async-start(), calls=%async_computation.5 | async-start | bytes 5570560 | tf_op jit(solution)/shard_map/reduce_scatter | solution.py:159
  343.7 67.5 %copy-start.16 = (f32[640]{0:T(1024)S(1)}, f32[640]{0:T(1024)}, u32[]{:S(2)}) copy-start(f32[640]{0:T(1024)} %param.30) | copy-start | bytes 7684
  343.7 230.6 %all-reduce.5.cloned.1.call-start = ((), (), s32[]{:S(2)}) async-start(), calls=%async_computation.8 | async-start | bytes 163840 | tf_op jit(solution)/shard_map/psum | solution.py:169
  414.9 219.7 %all-gather.9.cloned.1.call-start = ((), (), s32[]{:S(2)}) async-start(), calls=%async_computation.6 | async-start | bytes 5570560 | tf_op jit(solution)/shard_map/all_gather | solution.py:176
  577.4 64.1 %copy-start.5 = (bf16[16,2560]{1,0:T(8,128)(2,1)}, bf16[16,2560]{1,0:T(8,128)(2,1)S(1)}, u32[]{:S(2)}) copy-start(bf16[16,2560]{1,0:T(8,128)(2,1)S(1)} %add_convert_fusion.2) | copy-start | bytes 245764
  (4 other events, 3.0 us)
Sparse Core Ops, SparseCore 0:
  10.2 59.4 all-gather.4
  186.7 77.4 reduce-scatter.2
  269.0 56.6 all-gather.6
  329.4 78.6 all-reduce.2
  411.7 79.0 reduce-scatter.4
  494.8 79.4 all-reduce.4
  577.0 57.4 all-gather.8
where the time goes:
time: 650 us; the launch traced here: 648 us
  waiting for transfers between devices  410 us (63%)
  matrix products  92.4 us (14%)
  other arithmetic  82.2 us (13%)
  blocking collectives  33.2 us (5%)
  between operations  14.4 us (2%)
  local copies, waits for them, and re-layouts  14.1 us (2%)
    psum x1, waiting for transfers between devices, per_device(): lax.psum(jnp.dot(dec_hidden, w_down, preferred_element_type=jnp.float32)....  78.8 us
    reduce_scatter x1, waiting for transfers between devices, per_device(): lax.psum_scatter(jnp.dot(attn, w_out, preferred_element_type=jnp.float32)...  76.8 us
    reduce_scatter x1, waiting for transfers between devices, per_device(): lax.psum_scatter(jnp.dot(hidden, w_down, preferred_element_type=jnp.float...  75.9 us
    psum x1, waiting for transfers between devices, per_device(): lax.psum(jnp.dot(dec_attn, w_out, preferred_element_type=jnp.float32).ast...  64.3 us
    all_gather x1, waiting for transfers between devices, per_device(): lax.all_gather(x_pre, 'tensor', axis=0, tiled=True)  58 us
    all_gather x1, waiting for transfers between devices, per_device(): lax.all_gather(layer_out, 'tensor', axis=0, tiled=True)  54 us
    sub x2, other arithmetic, attend_block(): weights = jnp.where(mask[None], jnp.exp(scores - highest), 0.0)  50.8 us
    all_gather x3, blocking collectives, combined_all(): pieces = jax.tree.map(lambda part: lax.all_gather(part, axis), value)  33.2 us
  transfers between devices with their start and end apart: 7, of which 7 were waited for; matrix products, arithmetic and copies ran while one was open for 9% of the time, Pallas kernels for 0%

commit v1 on v0

--- a/solution.py
+++ b/solution.py
@@ -146,8 +146,12 @@
         scatter_dimension=0,
         tiled=True,
     ).astype(jnp.float32)
-    dec_sum = lax.psum(
-        jnp.dot(dec_attn, w_out, preferred_element_type=jnp.float32).astype(jnp.bfloat16), "tensor"
+    dec_sum = jnp.sum(
+        lax.all_gather(
+            jnp.dot(dec_attn, w_out, preferred_element_type=jnp.float32).astype(jnp.bfloat16),
+            "tensor",
+        ),
+        axis=0,
     ).astype(jnp.float32)
     h_first = layer_norm(
         x_pre.astype(jnp.float32) + attn_part + biases[0], gains[0], shifts[0]

time: 650 us -> 610 us (0.938)
  waiting for transfers between devices: 410 us -> 374 us
    psum x1 -> x0, waiting for transfers between devices: 64.3 us -> none  [per_device(): lax.psum(jnp.dot(dec_attn, w_out, preferred_element_type=jnp.float32).ast...]
    all_gather x0 -> x1, waiting for transfers between devices: none -> 26.7 us  [per_device(): lax.all_gather(jnp.dot(dec_attn, w_out, preferred_element_type=jnp.float3...]
  transfers between devices with their start and end apart: 7 -> 7, of which waited for: 7 -> 7; matrix products, arithmetic and copies ran while one was open for 9% -> 10% of each run, Pallas kernels for 0% -> 0%
where the time goes in v1:
time: 610 us; the launch traced here: 609 us
  waiting for transfers between devices  374 us (61%)
  matrix products  92.4 us (15%)
  other arithmetic  80.4 us (13%)
  blocking collectives  33.1 us (5%)
  between operations  14.4 us (2%)
  local copies, waits for them, and re-layouts  13 us (2%)
    psum x1, waiting for transfers between devices, per_device(): lax.psum(jnp.dot(dec_hidden, w_down, preferred_element_type=jnp.float32)....  78.5 us
    reduce_scatter x1, waiting for transfers between devices, per_device(): lax.psum_scatter(jnp.dot(attn, w_out, preferred_element_type=jnp.float32)...  76.2 us
    reduce_scatter x1, waiting for transfers between devices, per_device(): lax.psum_scatter(jnp.dot(hidden, w_down, preferred_element_type=jnp.float...  74.8 us
    all_gather x1, waiting for transfers between devices, per_device(): lax.all_gather(x_pre, 'tensor', axis=0, tiled=True)  58 us
    all_gather x1, waiting for transfers between devices, per_device(): lax.all_gather(layer_out, 'tensor', axis=0, tiled=True)  54.2 us
    sub x2, other arithmetic, attend_block(): weights = jnp.where(mask[None], jnp.exp(scores - highest), 0.0)  50.8 us
    all_gather x3, blocking collectives, combined_all(): pieces = jax.tree.map(lambda part: lax.all_gather(part, axis), value)  33.1 us
    all_gather x1, waiting for transfers between devices, per_device(): lax.all_gather(jnp.dot(dec_attn, w_out, preferred_element_type=jnp.float3...  26.7 us
  transfers between devices with their start and end apart: 7, of which 7 were waited for; matrix products, arithmetic and copies ran while one was open for 10% of the time, Pallas kernels for 0%

profile of v1, /device:TPU:1, one launch (start us, length us, event | category | flops | bytes accessed | tf_op | source)
XLA Modules:
  0.0 609.1 jit_solution(6969164641392655972)
XLA Ops:
  8.0 3.7 fusion.182
  11.7 58.0 %all-gather.7.cloned.1.call-done = bf16[1024,2560]{1,0:T(8,128)(2,1)} async-done(((bf16[64,2560]{1,0:T(8,128)(2,1)}), bf16[1024,2560]{1,0:T(8,128)(2,1)}) %all-gather.7.cloned.1.call-update) | async-done | bytes 5242896 | tf_op jit(solution)/shard_map/all_gather | solution.py:88
  69.7 6.1 convolution_convert_fusion.5
  79.2 101.0 %while.24 = (s32[]{:T(128)}, bf16[2,512,2,80]{1,3,2,0:T(8,128)(2,1)}, s32[]{:T(128)}, s32[2]{0:T(128)S(1)}, s32[1024]{0:T(1024)S(1)}, /*index=5*/s32[1,1024]{1,0...) while((s32[]{:T(128)}, ...), condition=%wide.region_3.4_spmd, body=%wide.region_0.3_spmd.sunk | while | flops 1731291136 | bytes 107183400 | solution.py:141
  80.4 11.4 %fusion.215 = f32[2,512,5120]{2,1,0:T(8,128)} fusion(bf16[5120,2,80]{0,2,1:T(8,128)(2,1)} %get-tuple-element.300, bf16[1024,2,80]{0,2,1:T(8,128)(2,1)} %get-tuple-element.299, s32[]{:T(128)S(6)} %select_n.124), kind=kOutput, calls=%fused_computation.16.clone.1 | convolution fusion | flops 838860800 | bytes 22773764 | tf_op jit(solution)/shard_map/while/body/eval_jaxpr/qhd,khd->hqk/dot_general | solution.py:131
  94.7 25.4 %fusion.217 = (f32[2,512]{1,0:T(2,128)S(1)}, f32[2,512,5120]{2,1,0:T(8,128)}) fusion(f32[2,512,5120]{2,1,0:T(8,128)} %fusion.215, pred[512,5120]{1,0:T(8,128)(4,1)S(1)} %pad_add_fusion.2), kind=kOutput, calls=%fused_computation.273.clone.1 | output fusion | flops 36705280 | bytes 44568576 | tf_op jit(solution)/shard_map/while/body/eval_jaxpr/sub | solution.py:135
  120.1 8.8 %fusion.218 = bf16[2,512,2,80]{1,3,2,0:T(8,128)(2,1)S(1)} fusion(bf16[2,512,2,80]{1,3,2,0:T(8,128)(2,1)S(1)} %copy-done.6, s32[]{:T(128)S(6)} %copy.93, bf16[5120,2,80]{0,2,1:T(8,128)(2,1)S(1)} %copy-done.3, f32[2,512,5120]{2,1,0:T(8,128)} %get-tuple-element.254, f32[2,512]{1,0:T(2,128)S(1)} %get-tuple-element.255), kind=kOutput, calls=%fused_computation.15.clone.1 | convolution fusion | flops 849428480 | bytes 22777860 | tf_op jit(solution)/shard_map/while/body/eval_jaxpr/hqk,khd->qhd/dot_general | solution.py:137
  130.9 11.4 %fusion.215 = f32[2,512,5120]{2,1,0:T(8,128)} fusion(bf16[5120,2,80]{0,2,1:T(8,128)(2,1)} %get-tuple-element.300, bf16[1024,2,80]{0,2,1:T(8,128)(2,1)} %get-tuple-element.299, s32[]{:T(128)S(6)} %select_n.124), kind=kOutput, calls=%fused_computation.16.clone.1 | convolution fusion | flops 838860800 | bytes 22773764 | tf_op jit(solution)/shard_map/while/body/eval_jaxpr/qhd,khd->hqk/dot_general | solution.py:131
  145.2 25.4 %fusion.217 = (f32[2,512]{1,0:T(2,128)S(1)}, f32[2,512,5120]{2,1,0:T(8,128)}) fusion(f32[2,512,5120]{2,1,0:T(8,128)} %fusion.215, pred[512,5120]{1,0:T(8,128)(4,1)S(1)} %pad_add_fusion.2), kind=kOutput, calls=%fused_computation.273.clone.1 | output fusion | flops 36705280 | bytes 44568576 | tf_op jit(solution)/shard_map/while/body/eval_jaxpr/sub | solution.py:135
  170.6 8.8 %fusion.218 = bf16[2,512,2,80]{1,3,2,0:T(8,128)(2,1)S(1)} fusion(bf16[2,512,2,80]{1,3,2,0:T(8,128)(2,1)S(1)} %copy-done.6, s32[]{:T(128)S(6)} %copy.93, bf16[5120,2,80]{0,2,1:T(8,128)(2,1)S(1)} %copy-done.3, f32[2,512,5120]{2,1,0:T(8,128)} %get-tuple-element.254, f32[2,512]{1,0:T(2,128)S(1)} %get-tuple-element.255), kind=kOutput, calls=%fused_computation.15.clone.1 | convolution fusion | flops 849428480 | bytes 22777860 | tf_op jit(solution)/shard_map/while/body/eval_jaxpr/hqk,khd->qhd/dot_general | solution.py:137
  181.5 5.0 convolution_convert_fusion.1
  188.0 76.2 %reduce-scatter.3.cloned.1.call-done = bf16[64,2560]{1,0:T(8,128)(2,1)} async-done(((bf16[1024,2560]{1,0:T(8,128)(2,1)}), bf16[64,2560]{1,0:T(8,128)(2,1)}) %reduce-scatter.3.cloned.1.call-update) | async-done | bytes 327696 | tf_op jit(solution)/shard_map/reduce_scatter | solution.py:143
  277.4 14.7 %all-gather = f32[128,2,80]{2,1,0:T(2,128)S(1)} all-gather(f32[16,2,80]{2,1,0:T(2,128)S(1)} %multiply_add_fusion), channel_id=2, replica_groups=mesh['rep'=8,'tensor'=16] {'rep'}, dimensions={0}, use_global_device_ids=true | all-gather | bytes 92160 | tf_op jit(solution)/shard_map/all_gather | solution.py:10
  292.9 10.3 %all_gather.32 = f32[8,16,2]{1,2,0:T(2,128)S(1)} all-gather(f32[1,16,2]{1,2,0:T(2,128)S(1)} %get-tuple-element.148), channel_id=1, replica_groups=mesh['rep'=8,'tensor'=16] {'rep'}, dimensions={0}, use_global_device_ids=true | all-gather | bytes 1152 | tf_op jit(solution)/shard_map/all_gather | solution.py:10
  303.2 8.1 %all_gather.33 = f32[8,16,2]{1,2,0:T(2,128)S(1)} all-gather(f32[1,16,2]{1,2,0:T(2,128)S(1)} %get-tuple-element.147), channel_id=1, replica_groups=mesh['rep'=8,'tensor'=16] {'rep'}, dimensions={0}, use_global_device_ids=true | all-gather | bytes 1152 | tf_op jit(solution)/shard_map/all_gather | solution.py:10
  311.3 7.4 %while.25 = (s32[]{:T(128)}, f32[16,2]{0,1:T(2,128)S(1)}, f32[16,2]{0,1:T(2,128)S(1)}, f32[16,2,80]{2,1,0:T(2,128)S(1)}, f32[7,16,2]{1,2,0:T(2,128)S(1)}, /*inde...) while((s32[]{:T(128)}, f32[16,2]{0,1:T(2,128)S(1)}, f32[16,2]{0,1:T(2,128)S(1)}, ...), condition=%wide.region_14.15_spmd, body=%wide.region_13.14_spmd.sunk | while | flops 7874 | bytes 32613 | solution.py:13
  321.2 4.6 all-gather.9.cloned.1.call-done
  325.8 17.9 %convolution_convert_fusion = bf16[1024,2560]{1,0:T(8,128)(2,1)} fusion(bf16[640,2560]{1,0:T(8,128)(2,1)S(1)} %copy-done, bf16[1024,2560]{1,0:T(8,128)(2,1)} %all-gather.9.cloned.1.call-done, bf16[2560,640]{1,0:T(8,128)(2,1)} %param.29, f32[640]{0:T(1024)S(1)} %copy-done.16), kind=kOutput, calls=%fused_computation.33 | convolution fusion | flops 6756761600 | bytes 17041920 | tf_op jit(solution)/shard_map/dot_general | solution.py:164
  343.7 26.7 %all-gather.13.cloned.1.call-done = bf16[256,2560]{1,0:T(8,128)(2,1)} async-done(((bf16[16,2560]{1,0:T(8,128)(2,1)}), bf16[256,2560]{1,0:T(8,128)(2,1)}) %all-gather.13.cloned.1.call-update) | async-done | bytes 1310736 | tf_op jit(solution)/shard_map/all_gather | solution.py:150
  373.2 3.6 convolution_convert_fusion.2
  376.9 74.8 %reduce-scatter.5.cloned.1.call-done = bf16[64,2560]{1,0:T(8,128)(2,1)} async-done(((bf16[1024,2560]{1,0:T(8,128)(2,1)}), bf16[64,2560]{1,0:T(8,128)(2,1)}) %reduce-scatter.5.cloned.1.call-update) | async-done | bytes 327696 | tf_op jit(solution)/shard_map/reduce_scatter | solution.py:163
  456.3 78.5 %all-reduce.2.cloned.1.call-done = bf16[16,2560]{1,0:T(8,128)(2,1)} async-done(((bf16[16,2560]{1,0:T(8,128)(2,1)}), bf16[16,2560]{1,0:T(8,128)(2,1)}) %all-reduce.2.cloned.1.call-update) | async-done | bytes 81936 | tf_op jit(solution)/shard_map/psum | solution.py:173
  541.1 54.2 %all-gather.11.cloned.1.call-done = bf16[1024,2560]{1,0:T(8,128)(2,1)} async-done(((bf16[64,2560]{1,0:T(8,128)(2,1)}), bf16[1024,2560]{1,0:T(8,128)(2,1)}) %all-gather.11.cloned.1.call-update) | async-done | bytes 5242896 | tf_op jit(solution)/shard_map/all_gather | solution.py:180
  595.3 6.9 %convolution_convert_fusion.4 = bf16[1024,480]{0,1:T(8,128)(2,1)} fusion(bf16[1024,2560]{1,0:T(8,128)(2,1)} %all-gather.11.cloned.1.call-done, bf16[2560,480]{0,1:T(8,128)(2,1)} %param.35), kind=kOutput, calls=%fused_computation.62 | convolution fusion | flops 2517073920 | bytes 8683520 | tf_op jit(solution)/shard_map/dot_general | solution.py:85
  (157 shorter events, 52.5 us)
Async XLA Ops:
  7.2 318.6 %copy-start = (bf16[640,2560]{1,0:T(8,128)(2,1)S(1)}, bf16[640,2560]{1,0:T(8,128)(2,1)}, u32[]{:S(2)}) copy-start(bf16[640,2560]{1,0:T(8,128)(2,1)} %param.31) | copy-start | bytes 9830404
  7.2 62.5 %all-gather.7.cloned.1.call-start = ((), (), s32[]{:S(2)}) async-start(), calls=%async_computation.2 | async-start | bytes 5570560 | tf_op jit(solution)/shard_map/all_gather | solution.py:88
  7.9 256.3 %reduce-scatter.3.cloned.1.call-start = ((), (), s32[]{:S(2)}) async-start(), calls=%async_computation.3 | async-start | bytes 5570560 | tf_op jit(solution)/shard_map/reduce_scatter | solution.py:143
  69.7 6.9 %copy-start.2 = (bf16[4096,2,80]{0,2,1:T(8,128)(2,1)S(1)}, bf16[4096,2,80]{0,2,1:T(8,128)(2,1)}, u32[]{:S(2)}) copy-start(bf16[4096,2,80]{0,2,1:T(8,128)(2,1)} %get-tuple-element.139) | copy-start | bytes 3932164
  75.7 1.4 copy-start.1
  77.2 2.0 copy-start.8
  94.6 25.4 %copy-start.3 = (bf16[5120,2,80]{0,2,1:T(8,128)(2,1)S(1)}, bf16[5120,2,80]{0,2,1:T(8,128)(2,1)}, u32[]{:S(2)}) copy-start(bf16[5120,2,80]{0,2,1:T(8,128)(2,1)} %get-tuple-element.301) | copy-start | bytes 4915204 | tf_op jit(solution)/shard_map/while
  94.7 25.4 %copy-start.6 = (bf16[2,512,2,80]{1,3,2,0:T(8,128)(2,1)S(1)}, bf16[2,512,2,80]{1,3,2,0:T(8,128)(2,1)}, u32[]{:S(2)}) copy-start(bf16[2,512,2,80]{1,3,2,0:T(8,128)(2,1)} %get-tuple-element.281) | copy-start | bytes 983044 | tf_op jit(solution)/shard_map/while
  145.1 25.4 %copy-start.3 = (bf16[5120,2,80]{0,2,1:T(8,128)(2,1)S(1)}, bf16[5120,2,80]{0,2,1:T(8,128)(2,1)}, u32[]{:S(2)}) copy-start(bf16[5120,2,80]{0,2,1:T(8,128)(2,1)} %get-tuple-element.301) | copy-start | bytes 4915204 | tf_op jit(solution)/shard_map/while
  145.1 25.4 %copy-start.6 = (bf16[2,512,2,80]{1,3,2,0:T(8,128)(2,1)S(1)}, bf16[2,512,2,80]{1,3,2,0:T(8,128)(2,1)}, u32[]{:S(2)}) copy-start(bf16[2,512,2,80]{1,3,2,0:T(8,128)(2,1)} %get-tuple-element.281) | copy-start | bytes 983044 | tf_op jit(solution)/shard_map/while
  186.5 0.8 copy-start.15
  186.6 82.6 %copy-start.4 = (bf16[16,2560]{1,0:T(8,128)(2,1)S(1)}, bf16[16,2560]{1,0:T(8,128)(2,1)}, u32[]{:S(2)}) copy-start(bf16[16,2560]{1,0:T(8,128)(2,1)} %param.21) | copy-start | bytes 245764
  186.6 139.2 %all-gather.9.cloned.1.call-start = ((), (), s32[]{:S(2)}) async-start(), calls=%async_computation.4 | async-start | bytes 5570560 | tf_op jit(solution)/shard_map/all_gather | solution.py:159
  188.0 83.6 %copy-start.11 = (f32[2560]{0:T(1024)}, f32[2560]{0:T(1024)S(1)}, u32[]{:S(2)}) copy-start(f32[2560]{0:T(1024)S(1)} %get-tuple-element.97) | copy-start | bytes 30724
  188.0 83.6 %copy-start.12 = (f32[2560]{0:T(1024)}, f32[2560]{0:T(1024)S(1)}, u32[]{:S(2)}) copy-start(f32[2560]{0:T(1024)S(1)} %get-tuple-element.151) | copy-start | bytes 30724
  264.2 7.8 %copy-start.17 = (s32[16]{0:T(128)S(1)}, s32[16]{0:T(128)}, u32[]{:S(2)}) copy-start(s32[16]{0:T(128)} %param.24) | copy-start | bytes 196
  268.9 101.5 %all-gather.13.cloned.1.call-start = ((), (), s32[]{:S(2)}) async-start(), calls=%async_computation.8 | async-start | bytes 1392640 | tf_op jit(solution)/shard_map/all_gather | solution.py:150
  274.7 51.1 %copy-start.16 = (f32[640]{0:T(1024)S(1)}, f32[640]{0:T(1024)}, u32[]{:S(2)}) copy-start(f32[640]{0:T(1024)} %param.30) | copy-start | bytes 7684
  321.1 130.5 %reduce-scatter.5.cloned.1.call-start = ((), (), s32[]{:S(2)}) async-start(), calls=%async_computation.5 | async-start | bytes 5570560 | tf_op jit(solution)/shard_map/reduce_scatter | solution.py:163
  343.7 191.1 %all-reduce.2.cloned.1.call-start = ((), (), s32[]{:S(2)}) async-start(), calls=%async_computation.7 | async-start | bytes 163840 | tf_op jit(solution)/shard_map/psum | solution.py:173
  373.2 81.1 %copy-start.9 = (f32[2560]{0:T(1024)S(1)}, f32[2560]{0:T(1024)}, u32[]{:S(2)}) copy-start(f32[2560]{0:T(1024)} %get-tuple-element.96) | copy-start | bytes 30724
  373.2 81.1 %copy-start.10 = (f32[2560]{0:T(1024)S(1)}, f32[2560]{0:T(1024)}, u32[]{:S(2)}) copy-start(f32[2560]{0:T(1024)} %get-tuple-element.152) | copy-start | bytes 30724
  376.8 218.5 %all-gather.11.cloned.1.call-start = ((), (), s32[]{:S(2)}) async-start(), calls=%async_computation.6 | async-start | bytes 5570560 | tf_op jit(solution)/shard_map/all_gather | solution.py:180
  537.9 64.3 %copy-start.5 = (bf16[16,2560]{1,0:T(8,128)(2,1)}, bf16[16,2560]{1,0:T(8,128)(2,1)S(1)}, u32[]{:S(2)}) copy-start(bf16[16,2560]{1,0:T(8,128)(2,1)S(1)} %add_convert_fusion.2) | copy-start | bytes 245764
  (4 other events, 3.0 us)
Sparse Core Ops, SparseCore 0:
  10.2 59.4 all-gather.6
  186.7 77.5 reduce-scatter.2
  269.0 56.6 all-gather.8
  328.3 42.0 all-gather.12
  373.7 77.9 reduce-scatter.4
  455.3 79.4 all-reduce.1
  537.7 57.4 all-gather.10
